TPU v7x, 256 devices: a whole 4x4x8 slice. The times are simulated.
256 devices in a mesh: section: 8 (over y, core), leaf: 32 (over x, z).
Axes of the slice: x: 4, y: 4, z: 8, core: 2. Of those that a mesh axis runs over, the one named last changes fastest.
Arguments:
- state_map: float32 [8, 512, 512], P('section'), may hold values from -0.05303301 to 1.053033
- input_map: float32 [8, 512, 256], P('section'), may hold values from -0.25 to 0.25
- cost_state: float32 [8, 1, 32, 512], P('section', None, 'leaf'), may hold values from 0.5 to 5
- cost_input: float32 [8, 1, 32, 256], P('section', None, 'leaf'), may hold values from 0.5 to 5
- terminal: float32 [8, 1, 32, 512], P('section', None, 'leaf'), may hold values from 0.5 to 5
- prob_num: int32 [8, 1, 32], P('section', None, 'leaf'), may hold values from 56 to 64
- crosses: int32 [8, 1, 32], P('section', None, 'leaf'), may hold values 0 or 1
- root_state_map: float32 [512, 512], replicated, may hold values from -0.05303301 to 1.053033
- root_input_map: float32 [512, 256], replicated, may hold values from -0.25 to 0.25
- root_cost_input: float32 [1, 256], replicated, may hold values from 0.5 to 5
- root_terminal: float32 [1, 512], replicated, may hold values from 0.5 to 5
Outputs:
- hessian: float32 [8, 1, 32, 512, 512], P('section', None, 'leaf')
- gain: float32 [8, 1, 32, 256, 512], P('section', None, 'leaf')
- root_gain: float32 [1, 256, 512], P(None, 'section')
Inputs may be any that keep to these rules, and one draw needn't show every extreme that they name: `prob_num`: branch probability numerators in 64ths.
All inputs are finite; a program needn't handle non-finite values. No bound on the sum of `crosses` on one device may be relied on, other than what follows from the above.
Results may differ from a plain program's by a relative error of at most 0.00021.
Values sent between devices are 32-bit elements; how exact they have to be, the bound alone decides.
A program may use at most 128 MiB of HBM per device.

v0:
```python
import jax
import jax.numpy as jnp
from jax import lax
from jax.sharding import PartitionSpec as P


def shifted(array, axis, by):
    length = lax.axis_size(axis)
    pairs = [(i, i + by) for i in range(length) if 0 <= i + by < length]
    return lax.ppermute(array, axis, pairs)


def passed_along(array, axis, by):
    length = lax.axis_size(axis)
    return lax.ppermute(array, axis, [(i, (i + by) % length) for i in range(length)])


def finish(hess_xx, hess_ux, hess_uu):
    precise = lax.Precision.HIGHEST
    factor = jnp.linalg.cholesky(hess_uu)
    scaled = lax.linalg.triangular_solve(factor, hess_ux, left_side=True, lower=True)
    feedback = -lax.linalg.triangular_solve(
        factor, scaled, left_side=True, lower=True, transpose_a=True
    )
    hessian = hess_xx - jnp.dot(scaled.T, scaled, precision=precise)
    return (hessian, feedback)


def riccati(expected, state_map, input_map, cost_state, cost_input):
    precise = lax.Precision.HIGHEST
    exp_state = jnp.dot(expected, state_map, precision=precise)
    exp_input = jnp.dot(expected, input_map, precision=precise)
    hess_xx = jnp.dot(state_map.T, exp_state, precision=precise) + jnp.diag(cost_state)
    hess_ux = jnp.dot(input_map.T, exp_state, precision=precise)
    hess_uu = jnp.dot(input_map.T, exp_input, precision=precise) + jnp.diag(cost_input)
    return finish(hess_xx, hess_ux, hess_uu)


def on_device(
    state_map,
    input_map,
    cost_state,
    cost_input,
    terminal,
    prob_num,
    crosses,
    root_state_map,
    root_input_map,
    root_cost_input,
    root_terminal,
):
    sections = lax.axis_size("section")
    section_row = lax.axis_index("section")
    group_index = lax.axis_index("leaf")
    fronts = cost_state.shape[1]
    state_dim = state_map.shape[1]
    controls = input_map.shape[2]
    root_rows = controls // sections
    local_state = state_map[0]
    local_input = input_map[0]
    zero_cost = jnp.zeros((state_dim,), jnp.float32)
    hess_out = jnp.zeros((fronts, state_dim, state_dim), jnp.float32)
    gain_out = jnp.zeros((fronts, controls, state_dim), jnp.float32)
    root_out = jnp.zeros((fronts, root_rows, state_dim), jnp.float32)
    incoming = jnp.zeros((state_dim, state_dim), jnp.float32)
    for moment in range(sections + fronts - 1):
        front_id = moment - (sections - 1 - section_row)
        active = (front_id >= 0) & (front_id < fronts)
        front_pick = jnp.clip(front_id, 0, fronts - 1)
        expected = jnp.diag(terminal[0, front_pick, 0]) + incoming

        def compute_node(buffers):
            hess_new, gain_new = riccati(
                expected,
                local_state,
                local_input,
                cost_state[0, front_pick, 0],
                cost_input[0, front_pick, 0],
            )
            return (
                lax.dynamic_update_index_in_dim(buffers[0], hess_new, front_pick, 0),
                lax.dynamic_update_index_in_dim(buffers[1], gain_new, front_pick, 0),
                hess_new,
            )

        def keep_buffers(buffers):
            return (buffers[0], buffers[1], jnp.zeros((state_dim, state_dim), jnp.float32))

        hess_out, gain_out, latest = lax.cond(
            active, compute_node, keep_buffers, (hess_out, gain_out)
        )
        weight = prob_num[0, front_pick, 0].astype(jnp.float32) / 64.0
        weighted = weight * latest
        if moment < sections + fronts - 2:
            cross_flag = crosses[0, front_pick, 0].astype(jnp.float32)
            arrived, arrived_flag = shifted(
                (weighted, jnp.reshape(cross_flag, (1,))), "section", -1
            )
            far_part = arrived_flag[0] * arrived
            own_part = arrived - far_part
            incoming = own_part + passed_along(far_part, "leaf", 1)
        if moment >= sections - 1:
            root_front = moment - (sections - 1)
            on_top = section_row == 0
            root_diag = jnp.where(
                on_top & (group_index == 0), jnp.diag(root_terminal[root_front]), 0.0
            )
            contrib = jnp.where(on_top, weighted, 0.0) + root_diag
            root_total = lax.psum(contrib, ("section", "leaf"))
            root_hess, root_feedback = riccati(
                root_total, root_state_map, root_input_map, zero_cost, root_cost_input[root_front]
            )
            mine = lax.dynamic_slice_in_dim(root_feedback, section_row * root_rows, root_rows, 0)
            root_out = root_out.at[root_front].set(mine)
    hessian = hess_out[None, :, None, :, :]
    gain = gain_out[None, :, None, :, :]
    return (hessian, gain, root_out)


def solution(mesh):
    in_specs = (
        P("section", None, None),
        P("section", None, None),
        P("section", None, "leaf", None),
        P("section", None, "leaf", None),
        P("section", None, "leaf", None),
        P("section", None, "leaf"),
        P("section", None, "leaf"),
        P(),
        P(),
        P(),
        P(),
    )
    out_specs = (
        P("section", None, "leaf", None, None),
        P("section", None, "leaf", None, None),
        P(None, "section", None),
    )
    return jax.shard_map(
        on_device, mesh=mesh, in_specs=in_specs, out_specs=out_specs, check_vma=False
    )
```

profile of v0, /device:TPU:2, one launch (start us, length us, event | category | flops | bytes accessed | tf_op | source)
XLA Modules:
  0.0 1279.2 jit_solution(13759649830042761843)
XLA Ops:
  9.6 12.6 conditional.8
  26.8 2.4 collective-permute-done.1
  29.2 1.9 broadcast_multiply_fusion.6
  31.1 1.9 collective-permute-start.2
  33.0 18.1 %collective-permute-done.2 = f32[512,512]{0,1:T(8,128)} collective-permute-done((f32[512,512]{0,1:T(8,128)}, f32[512,512]{0,1:T(8,128)}, u32[]{:S(2)}, u32[]{:S(2)}) %collective-permute-start.2) | collective-permute-done | bytes 1048608 | tf_op jit(solution)/shard_map/ppermute | solution.py:15
  51.0 10.4 conditional.9
  61.5 1.3 broadcast_multiply_fusion.12
  64.1 12.8 collective-permute-done.3
  76.9 1.8 broadcast_multiply_fusion.5
  78.6 17.2 %collective-permute-done.4 = f32[512,512]{0,1:T(8,128)} collective-permute-done((f32[512,512]{0,1:T(8,128)}, f32[512,512]{0,1:T(8,128)}, u32[]{:S(2)}, u32[]{:S(2)}) %collective-permute-start.4) | collective-permute-done | bytes 1048608 | tf_op jit(solution)/shard_map/ppermute | solution.py:15
  95.9 10.7 conditional.10
  106.6 1.3 broadcast_multiply_fusion.11
  109.2 21.2 %collective-permute-done.5 = f32[512,512]{0,1:T(8,128)S(1)} collective-permute-done((f32[512,512]{0,1:T(8,128)S(1)}, f32[512,512]{0,1:T(8,128)S(1)}, u32[]{:S(2)}, u32[]{:S(2)}) %collective-permute-start.5) | collective-permute-done | bytes 1048608 | tf_op jit(solution)/shard_map/ppermute | solution.py:10
  130.4 1.8 broadcast_multiply_fusion.4
  132.2 17.2 %collective-permute-done.6 = f32[512,512]{0,1:T(8,128)} collective-permute-done((f32[512,512]{0,1:T(8,128)}, f32[512,512]{0,1:T(8,128)}, u32[]{:S(2)}, u32[]{:S(2)}) %collective-permute-start.6) | collective-permute-done | bytes 1048608 | tf_op jit(solution)/shard_map/ppermute | solution.py:15
  149.4 10.7 conditional.11
  160.1 1.3 broadcast_multiply_fusion.10
  162.8 22.2 %collective-permute-done.7 = f32[512,512]{0,1:T(8,128)S(1)} collective-permute-done((f32[512,512]{0,1:T(8,128)S(1)}, f32[512,512]{0,1:T(8,128)S(1)}, u32[]{:S(2)}, u32[]{:S(2)}) %collective-permute-start.7) | collective-permute-done | bytes 1048608 | tf_op jit(solution)/shard_map/ppermute | solution.py:10
  184.9 1.8 broadcast_multiply_fusion.3
  186.7 17.2 %collective-permute-done.8 = f32[512,512]{0,1:T(8,128)} collective-permute-done((f32[512,512]{0,1:T(8,128)}, f32[512,512]{0,1:T(8,128)}, u32[]{:S(2)}, u32[]{:S(2)}) %collective-permute-start.8) | collective-permute-done | bytes 1048608 | tf_op jit(solution)/shard_map/ppermute | solution.py:15
  204.0 10.7 conditional.12
  214.7 1.3 broadcast_multiply_fusion.9
  217.3 21.4 %collective-permute-done.9 = f32[512,512]{0,1:T(8,128)S(1)} collective-permute-done((f32[512,512]{0,1:T(8,128)S(1)}, f32[512,512]{0,1:T(8,128)S(1)}, u32[]{:S(2)}, u32[]{:S(2)}) %collective-permute-start.9) | collective-permute-done | bytes 1048608 | tf_op jit(solution)/shard_map/ppermute | solution.py:10
  238.7 1.8 broadcast_multiply_fusion.2
  240.5 17.2 %collective-permute-done.10 = f32[512,512]{0,1:T(8,128)} collective-permute-done((f32[512,512]{0,1:T(8,128)}, f32[512,512]{0,1:T(8,128)}, u32[]{:S(2)}, u32[]{:S(2)}) %collective-permute-start.10) | collective-permute-done | bytes 1048608 | tf_op jit(solution)/shard_map/ppermute | solution.py:15
  257.7 10.7 conditional.13
  268.4 1.3 broadcast_multiply_fusion.8
  271.1 14.1 %collective-permute-done.11 = f32[512,512]{0,1:T(8,128)S(1)} collective-permute-done((f32[512,512]{0,1:T(8,128)S(1)}, f32[512,512]{0,1:T(8,128)S(1)}, u32[]{:S(2)}, u32[]{:S(2)}) %collective-permute-start.11) | collective-permute-done | bytes 1048608 | tf_op jit(solution)/shard_map/ppermute | solution.py:10
  285.1 1.8 broadcast_multiply_fusion.1
  286.9 17.2 %collective-permute-done.12 = f32[512,512]{0,1:T(8,128)} collective-permute-done((f32[512,512]{0,1:T(8,128)}, f32[512,512]{0,1:T(8,128)}, u32[]{:S(2)}, u32[]{:S(2)}) %collective-permute-start.12) | collective-permute-done | bytes 1048608 | tf_op jit(solution)/shard_map/ppermute | solution.py:15
  304.1 10.7 conditional.14
  314.9 1.3 broadcast_multiply_fusion.7
  317.5 514.3 %collective-permute-done.13 = f32[512,512]{0,1:T(8,128)S(1)} collective-permute-done((f32[512,512]{0,1:T(8,128)S(1)}, f32[512,512]{0,1:T(8,128)S(1)}, u32[]{:S(2)}, u32[]{:S(2)}) %collective-permute-start.13) | collective-permute-done | bytes 1048608 | tf_op jit(solution)/shard_map/ppermute | solution.py:10
  831.7 1.8 broadcast_multiply_fusion
  833.5 17.2 %collective-permute-done.14 = f32[512,512]{0,1:T(8,128)} collective-permute-done((f32[512,512]{0,1:T(8,128)}, f32[512,512]{0,1:T(8,128)}, u32[]{:S(2)}, u32[]{:S(2)}) %collective-permute-start.14) | collective-permute-done | bytes 1048608 | tf_op jit(solution)/shard_map/ppermute | solution.py:15
  850.7 88.7 %conditional.15 = (f32[1,512,512]{1,2,0:T(8,128)}, f32[1,256,512]{2,1,0:T(8,128)}, f32[512,512]{0,1:T(8,128)S(1)}) conditional(s32[]{:T(128)} %convert_element_type.22, (f32[1,512,512]{1,2,0:T(8,128)}, f32[1,256,512]{2,1,0:T(8,128)}) %tuple.109, (f32[512,512]{0,1:T(8,128)}, f32[512,512]{1,0:T(8,128)S(1)}, f32[1,1,1,512]{3,2,1,0:T(1,128)S(1)}, ...), branch_computations={%region_18.22_spmd, %region_19.23_spmd} | conditional | flops 6697206272 | bytes 42669304 | solution.py:89
  850.7 2.6 copy.55
  853.3 2.6 copy.56
  855.9 2.5 copy.57
  858.4 2.6 copy.58
  861.0 2.7 fusion.134
  865.8 11.7 cholesky.662
  877.6 9.8 custom-call.59
  887.9 12.1 cholesky.679
  902.2 4.0 while.44
  902.8 1.4 bitcast_dynamic-update-slice_fusion.19
  904.8 1.4 bitcast_dynamic-update-slice_fusion.19
  906.1 19.7 %custom-call.60 = f32[2,128,128]{1,2,0:T(8,128)S(1)} custom-call(f32[2,128,128]{2,1,0:T(8,128)S(1)} %get-tuple-element.498), custom_call_target="InvertDiagBlocksLowerTriangular" | custom-call | tf_op jit(solution)/shard_map/cond/branch_1_fun/triangular_solve/custom-call.0 | solution.py:21
  925.8 3.1 fusion.190
  928.9 1.8 convolution_bitcast_fusion.22
  934.2 1.8 fusion.132
  936.0 2.1 convolution_subtract_fusion.28
  941.4 2.6 copy.59
  944.0 256.6 %all-reduce.3.cloned.1.call-done = f32[512,512]{0,1:T(8,128)} async-done(((f32[512,512]{0,1:T(8,128)}), f32[512,512]{0,1:T(8,128)}) %all-reduce.3.cloned.1.call-update) | async-done | bytes 1048592 | tf_op jit(solution)/shard_map/psum | solution.py:109
  1200.6 3.0 fusion.192
  1205.5 11.7 cholesky.696
  1217.3 9.8 custom-call.62
  1227.6 11.9 cholesky.713
  1241.6 3.9 while.45
  1242.2 1.3 bitcast_dynamic-update-slice_fusion.18
  1244.1 1.3 bitcast_dynamic-update-slice_fusion.18
  1245.5 19.7 %custom-call.64 = f32[2,128,128]{1,2,0:T(8,128)S(1)} custom-call(f32[2,128,128]{2,1,0:T(8,128)S(1)} %get-tuple-element.501), custom_call_target="InvertDiagBlocksLowerTriangular" | custom-call | tf_op jit(solution)/shard_map/triangular_solve/custom-call.4 | solution.py:22
  1265.2 1.8 fusion.193
  1267.1 1.8 convolution_bitcast_fusion.24
  (119 shorter events, 42.1 us)
Async XLA Ops:
  7.2 1258.0 %copy-start = (f32[512,512]{1,0:T(8,128)S(1)}, f32[512,512]{1,0:T(8,128)}, u32[]{:S(2)}) copy-start(f32[512,512]{1,0:T(8,128)} %param.41) | copy-start | bytes 3145732
  7.2 1193.4 %all-reduce.3.cloned.1.call-start = ((), (), s32[]{:S(2)}) async-start(), calls=%async_computation | async-start | bytes 2097152 | tf_op jit(solution)/shard_map/psum | solution.py:109
  7.2 0.8 copy-start.24
  8.0 1.1 copy-start.1
  8.1 1.5 copy-start.4
  8.9 0.7 copy-start.22
  8.9 0.7 copy-start.23
  23.6 5.6 collective-permute-start
  25.5 3.7 collective-permute-start.1
  29.2 1.9 copy-start.15
  29.2 21.9 %copy-start.2 = (f32[1,512,512]{2,1,0:T(8,128)S(1)}, f32[1,512,512]{2,1,0:T(8,128)}, u32[]{:S(2)}) copy-start(f32[1,512,512]{2,1,0:T(8,128)} %param.34) | copy-start | bytes 3145732
  31.1 20.0 %collective-permute-start.2 = (f32[512,512]{0,1:T(8,128)}, f32[512,512]{0,1:T(8,128)}, u32[]{:S(2)}, u32[]{:S(2)}) collective-permute-start(f32[512,512]{0,1:T(8,128)} %broadcast_multiply_fusion.6), channel_id=1, source_target_pairs={{0,1},{1,2},{2,3},{3,4},{4,5},{5,6},{6,7},{7,8},{8,9},{9,10},{10,1... | collective-permute-start | bytes 3145736 | tf_op jit(solution)/shard_map/ppermute | solution.py:15
  62.8 14.1 %collective-permute-start.3 = (f32[512,512]{0,1:T(8,128)S(1)}, f32[512,512]{0,1:T(8,128)S(1)}, u32[]{:S(2)}, u32[]{:S(2)}) collective-permute-start(f32[512,512]{0,1:T(8,128)S(1)} %broadcast_multiply_fusion.12), channel_id=1, source_target_pairs={{32,0},{64,32},{96,64},{128,96},{160,128},{192,160},{224,192},{33,... | collective-permute-start | bytes 3145736 | tf_op jit(solution)/shard_map/ppermute | solution.py:10
  76.9 1.8 copy-start.18
  78.6 17.2 %collective-permute-start.4 = (f32[512,512]{0,1:T(8,128)}, f32[512,512]{0,1:T(8,128)}, u32[]{:S(2)}, u32[]{:S(2)}) collective-permute-start(f32[512,512]{0,1:T(8,128)} %broadcast_multiply_fusion.5), channel_id=1, source_target_pairs={{0,1},{1,2},{2,3},{3,4},{4,5},{5,6},{6,7},{7,8},{8,9},{9,10},{10,1... | collective-permute-start | bytes 3145736 | tf_op jit(solution)/shard_map/ppermute | solution.py:15
  107.9 22.5 %collective-permute-start.5 = (f32[512,512]{0,1:T(8,128)S(1)}, f32[512,512]{0,1:T(8,128)S(1)}, u32[]{:S(2)}, u32[]{:S(2)}) collective-permute-start(f32[512,512]{0,1:T(8,128)S(1)} %broadcast_multiply_fusion.11), channel_id=1, source_target_pairs={{32,0},{64,32},{96,64},{128,96},{160,128},{192,160},{224,192},{33,... | collective-permute-start | bytes 3145736 | tf_op jit(solution)/shard_map/ppermute | solution.py:10
  130.4 1.8 copy-start.19
  132.2 17.2 %collective-permute-start.6 = (f32[512,512]{0,1:T(8,128)}, f32[512,512]{0,1:T(8,128)}, u32[]{:S(2)}, u32[]{:S(2)}) collective-permute-start(f32[512,512]{0,1:T(8,128)} %broadcast_multiply_fusion.4), channel_id=1, source_target_pairs={{0,1},{1,2},{2,3},{3,4},{4,5},{5,6},{6,7},{7,8},{8,9},{9,10},{10,1... | collective-permute-start | bytes 3145736 | tf_op jit(solution)/shard_map/ppermute | solution.py:15
  161.5 23.5 %collective-permute-start.7 = (f32[512,512]{0,1:T(8,128)S(1)}, f32[512,512]{0,1:T(8,128)S(1)}, u32[]{:S(2)}, u32[]{:S(2)}) collective-permute-start(f32[512,512]{0,1:T(8,128)S(1)} %broadcast_multiply_fusion.10), channel_id=1, source_target_pairs={{32,0},{64,32},{96,64},{128,96},{160,128},{192,160},{224,192},{33,... | collective-permute-start | bytes 3145736 | tf_op jit(solution)/shard_map/ppermute | solution.py:10
  184.9 1.8 copy-start.20
  186.7 17.2 %collective-permute-start.8 = (f32[512,512]{0,1:T(8,128)}, f32[512,512]{0,1:T(8,128)}, u32[]{:S(2)}, u32[]{:S(2)}) collective-permute-start(f32[512,512]{0,1:T(8,128)} %broadcast_multiply_fusion.3), channel_id=1, source_target_pairs={{0,1},{1,2},{2,3},{3,4},{4,5},{5,6},{6,7},{7,8},{8,9},{9,10},{10,1... | collective-permute-start | bytes 3145736 | tf_op jit(solution)/shard_map/ppermute | solution.py:15
  216.0 22.7 %collective-permute-start.9 = (f32[512,512]{0,1:T(8,128)S(1)}, f32[512,512]{0,1:T(8,128)S(1)}, u32[]{:S(2)}, u32[]{:S(2)}) collective-permute-start(f32[512,512]{0,1:T(8,128)S(1)} %broadcast_multiply_fusion.9), channel_id=1, source_target_pairs={{32,0},{64,32},{96,64},{128,96},{160,128},{192,160},{224,192},{33,... | collective-permute-start | bytes 3145736 | tf_op jit(solution)/shard_map/ppermute | solution.py:10
  238.7 1.8 copy-start.21
  240.5 17.2 %collective-permute-start.10 = (f32[512,512]{0,1:T(8,128)}, f32[512,512]{0,1:T(8,128)}, u32[]{:S(2)}, u32[]{:S(2)}) collective-permute-start(f32[512,512]{0,1:T(8,128)} %broadcast_multiply_fusion.2), channel_id=1, source_target_pairs={{0,1},{1,2},{2,3},{3,4},{4,5},{5,6},{6,7},{7,8},{8,9},{9,10},{10,1... | collective-permute-start | bytes 3145736 | tf_op jit(solution)/shard_map/ppermute | solution.py:15
  269.8 15.4 %collective-permute-start.11 = (f32[512,512]{0,1:T(8,128)S(1)}, f32[512,512]{0,1:T(8,128)S(1)}, u32[]{:S(2)}, u32[]{:S(2)}) collective-permute-start(f32[512,512]{0,1:T(8,128)S(1)} %broadcast_multiply_fusion.8), channel_id=1, source_target_pairs={{32,0},{64,32},{96,64},{128,96},{160,128},{192,160},{224,192},{33,... | collective-permute-start | bytes 3145736 | tf_op jit(solution)/shard_map/ppermute | solution.py:10
  285.1 1.8 copy-start.17
  286.9 17.2 %collective-permute-start.12 = (f32[512,512]{0,1:T(8,128)}, f32[512,512]{0,1:T(8,128)}, u32[]{:S(2)}, u32[]{:S(2)}) collective-permute-start(f32[512,512]{0,1:T(8,128)} %broadcast_multiply_fusion.1), channel_id=1, source_target_pairs={{0,1},{1,2},{2,3},{3,4},{4,5},{5,6},{6,7},{7,8},{8,9},{9,10},{10,1... | collective-permute-start | bytes 3145736 | tf_op jit(solution)/shard_map/ppermute | solution.py:15
  316.2 515.6 %collective-permute-start.13 = (f32[512,512]{0,1:T(8,128)S(1)}, f32[512,512]{0,1:T(8,128)S(1)}, u32[]{:S(2)}, u32[]{:S(2)}) collective-permute-start(f32[512,512]{0,1:T(8,128)S(1)} %broadcast_multiply_fusion.7), channel_id=1, source_target_pairs={{32,0},{64,32},{96,64},{128,96},{160,128},{192,160},{224,192},{33,... | collective-permute-start | bytes 3145736 | tf_op jit(solution)/shard_map/ppermute | solution.py:10
  831.7 1.8 copy-start.16
  833.5 17.2 %collective-permute-start.14 = (f32[512,512]{0,1:T(8,128)}, f32[512,512]{0,1:T(8,128)}, u32[]{:S(2)}, u32[]{:S(2)}) collective-permute-start(f32[512,512]{0,1:T(8,128)} %broadcast_multiply_fusion), channel_id=1, source_target_pairs={{0,1},{1,2},{2,3},{3,4},{4,5},{5,6},{6,7},{7,8},{8,9},{9,10},{10,1... | collective-permute-start | bytes 3145736 | tf_op jit(solution)/shard_map/ppermute | solution.py:15
  863.6 1.0 copy-start.12
  939.5 0.7 copy-start.25
  941.4 259.2 %copy-start.13 = (f32[512,256]{1,0:T(8,128)S(1)}, f32[512,256]{1,0:T(8,128)}, u32[]{:S(2)}) copy-start(f32[512,256]{1,0:T(8,128)} %param.42) | copy-start | bytes 1572868
  1203.6 0.7 copy-start.26
  1217.3 47.9 %copy-start.14 = (f32[512,512]{0,1:T(8,128)S(1)}, f32[512,512]{0,1:T(8,128)}, u32[]{:S(2)}) copy-start(f32[512,512]{0,1:T(8,128)} %all-reduce.3.cloned.1.call-done) | copy-start | bytes 3145732
Sparse Core Ops, SparseCore 0:
  941.5 259.0 all-reduce.2
where the time goes:
time: 1290 us; the launch traced here: 1280 us
  waiting for transfers between devices  986 us (76%)
  other arithmetic  135 us (10%)
  loops' own time  68.3 us (5%)
  local copies, waits for them, and re-layouts  35 us (3%)
  matrix products  24.6 us (2%)
  between operations  17.4 us (1%)
    ppermute x8, waiting for transfers between devices, shifted(): return lax.ppermute(array, axis, pairs)  608 us
    psum x1, waiting for transfers between devices, on_device(): root_total = lax.psum(contrib, ('section', 'leaf'))  257 us
    ppermute x7, waiting for transfers between devices, passed_along(): lax.ppermute(array, axis, [(i, (i + by) % length) for i in range(length)])  121 us
    another operation x12, other arithmetic, finish(): factor = jnp.linalg.cholesky(hess_uu)  68.6 us
    another operation x8, loops' own time, on_device(): lax.cond(active, compute_node, keep_buffers, (hess_out, gain_out))  68.3 us
  transfers between devices with their start and end apart: 16, of which 15 were waited for; matrix products, arithmetic and copies ran while one was open for 0% of the time, Pallas kernels for 0%

commit v1 on v0

v1 whole, which is shorter than its diff:
```python
import functools

import jax
import jax.numpy as jnp
from jax import lax
from jax.experimental import pallas as pl
from jax.experimental.pallas import tpu as pltpu
from jax.sharding import PartitionSpec as P

F32, BF16 = jnp.float32, jnp.bfloat16
MESH = pl.DeviceIdType.MESH
VMEM = pltpu.VMEM
CONTRACT = (((1,), (0,)), ((), ()))
CONTRACT_ROWS = (((0,), (0,)), ((), ()))


def split(x):
    high = x.astype(BF16)
    return high, (x - high.astype(F32)).astype(BF16)


def dot_one(a, b, dims=CONTRACT):
    return lax.dot_general(a, b, dims, preferred_element_type=F32)


def dot_split(a, b, dims=CONTRACT):
    return dot_one(a[0], b[0], dims) + (dot_one(a[0], b[1], dims) + dot_one(a[1], b[0], dims))


def dot3(a, b, dims=CONTRACT):
    return dot_split(split(a), split(b), dims)


def lanes(x, j):
    return jnp.broadcast_to(x[:, j : j + 1], (8, 128))


def rows(x, k):
    return jnp.broadcast_to(x[k : k + 1, :], (8, 128))


def inverse128(a):
    groups = 16
    lane = lax.broadcasted_iota(jnp.int32, (8, 128), 1)
    row = lax.broadcasted_iota(jnp.int32, (8, 128), 0)
    masks = [row == k for k in range(8)]
    held = [a[8 * g : 8 * g + 8, :] for g in range(groups)]
    for t in range(groups):
        off = 8 * t
        inside = (lane >= off) & (lane < off + 8)
        top = held[t]
        cols = [lanes(top, off + j) for j in range(8)]
        top = jnp.where(inside, jnp.where(lane - off == row, 1.0, 0.0), top)
        for k in range(8):
            pivot = 1.0 / rows(cols[k], k)
            lead = rows(top, k) * pivot
            factor = jnp.where(masks[k], 0.0, cols[k])
            top = jnp.where(masks[k], lead, top - factor * lead)
            for j in range(k + 1, 8):
                lead_j = rows(cols[j], k) * pivot
                cols[j] = jnp.where(masks[k], lead_j, cols[j] - factor * lead_j)
        out = [jnp.where(inside, 0.0, held[g]) for g in range(groups)]
        for k in range(8):
            lead = rows(top, k)
            for g in range(groups):
                if g != t:
                    out[g] = out[g] - lanes(held[g], off + k) * lead
        out[t] = top
        held = out
    return jnp.concatenate(held, axis=0)


def solve(huu, hux, inv):
    a12, a21 = huu[0:128, 128:256], huu[128:256, 0:128]
    hux1 = hux[0:128]
    first = split(inv(huu[0:128, 0:128]))
    t12 = dot_split(first, split(a12))
    th = dot_split(first, split(hux1))
    a21s = split(a21)
    second = split(inv(huu[128:256, 128:256] - dot_split(a21s, split(t12))))
    rest = hux[128:256] - dot_split(a21s, split(th))
    g2 = dot_split(second, split(rest))
    g1 = th - dot3(t12, g2)
    return hux1, th, rest, g2, g1


def eye_times(vector, size):
    r = lax.broadcasted_iota(jnp.int32, (size, size), 0)
    c = lax.broadcasted_iota(jnp.int32, (size, size), 1)
    return jnp.where(r == c, jnp.broadcast_to(vector, (size, size)), 0.0)


def chain_kernel(
    sections, groups, prob, crosses, state_map, input_map, cost_state, cost_input, terminal,
    hess_ref, gain_ref,
    own_in, far_in, own_out, far_out,
    m_s, n_s, mt_s, nt_s, e_s, ym_s, yn_s, hux_ref, z_ref, x_ref, inv_ref,
    own_send, own_recv, far_send, far_recv,
):
    s = lax.axis_index("section")
    g = lax.axis_index("leaf")
    up, down = lax.rem(s + sections - 1, sections), lax.rem(s + 1, sections)
    after, before = lax.rem(g + 1, groups), lax.rem(g + groups - 1, groups)
    parents = ({"section": up, "leaf": g}, {"section": up, "leaf": after})
    children = ({"section": down, "leaf": g}, {"section": down, "leaf": before})

    barrier = pltpu.get_barrier_semaphore()
    for other in parents + children:
        pl.semaphore_signal(barrier, inc=1, device_id=other, device_id_type=MESH)
    pl.semaphore_wait(barrier, 4)

    def slabs(src, dst, send, recv, device):
        out = []
        for i in range(4):
            part = (pl.ds(128 * i, 128), pl.ds(0, 128 * (i + 1)))
            out.append(
                pltpu.make_async_remote_copy(
                    src_ref=src.at[part], dst_ref=dst.at[part], send_sem=send.at[i], recv_sem=recv.at[i],
                    device_id=device, device_id_type=MESH,
                )
            )
        return out

    own_copies = slabs(own_out, own_in, own_send, own_recv, parents[0])
    far_copies = slabs(far_out, far_in, far_send, far_recv, parents[1])

    for i in range(4):
        block = slice(128 * i, 128 * (i + 1))
        value = state_map[block, :]
        m_s[0, block, :], m_s[1, block, :] = split(value)
        mt_s[0, :, block], mt_s[1, :, block] = split(value.T)
        value = input_map[block, :]
        n_s[0, block, :], n_s[1, block, :] = split(value)
        nt_s[0, :, block], nt_s[1, :, block] = split(value.T)

    @pl.when(s == sections - 1)
    def _():
        own_in[...] = jnp.zeros_like(own_in)
        far_in[...] = jnp.zeros_like(far_in)

    for i in range(4):
        @pl.when(s < sections - 1)
        def _():
            far_copies[i].wait_recv()
            own_copies[i].wait_recv()

        rowb = slice(128 * i, 128 * (i + 1))
        for j in range(i + 1):
            colb = slice(128 * j, 128 * (j + 1))
            block = own_in[rowb, colb] + far_in[rowb, colb]
            if i == j:
                block = block + eye_times(terminal[0:1, rowb], 128)
            e_s[0, rowb, colb], e_s[1, rowb, colb] = split(block)
            if i != j:
                e_s[0, colb, rowb], e_s[1, colb, rowb] = split(block.T)

    e = (e_s[0], e_s[1])
    yn_s[0], yn_s[1] = split(dot_split(e, (n_s[0], n_s[1])))
    for j in range(2):
        colb = slice(256 * j, 256 * (j + 1))
        ym_s[0, :, colb], ym_s[1, :, colb] = split(dot_split(e, (m_s[0, :, colb], m_s[1, :, colb])))
    nt, mt = (nt_s[0], nt_s[1]), (mt_s[0], mt_s[1])
    huu = dot_split(nt, (yn_s[0], yn_s[1])) + eye_times(cost_input[0:1, :], 256)
    for j in range(2):
        colb = slice(256 * j, 256 * (j + 1))
        ym = (ym_s[0, :, colb], ym_s[1, :, colb])
        hux_ref[:, colb] = dot_split(nt, ym)
        hess_ref[:, colb] = dot_split(mt, ym)
    for i in range(4):
        block = slice(128 * i, 128 * (i + 1))
        hess_ref[block, block] = hess_ref[block, block] + eye_times(cost_state[0:1, block], 128)

    def inv(a):
        return inverse128(a)

    hux1, th, rest, g2, g1 = solve(huu, hux_ref[...], inv)
    x_ref[0, 0:128, :], x_ref[1, 0:128, :] = split(hux1)
    x_ref[0, 128:256, :], x_ref[1, 128:256, :] = split(rest)
    z_ref[0, 0:128, :], z_ref[1, 0:128, :] = split(th)
    z_ref[0, 128:256, :], z_ref[1, 128:256, :] = split(g2)
    weight = prob[0].astype(F32) / 64.0
    crossing = crosses[0].astype(F32)
    far_weight = weight * crossing
    own_weight = weight - far_weight
    for j in range(2):
        colb = slice(256 * j, 256 * (j + 1))
        z = (z_ref[0, :, colb], z_ref[1, :, colb])
        hess_ref[:, colb] = hess_ref[:, colb] - dot_split((x_ref[0], x_ref[1]), z, CONTRACT_ROWS)

    for i in range(4):
        rowb = slice(128 * i, 128 * (i + 1))
        colb = slice(0, 128 * (i + 1))
        value = hess_ref[rowb, colb]
        far_out[rowb, colb] = value * far_weight
        own_out[rowb, colb] = value * own_weight

        @pl.when(s > 0)
        def _():
            far_copies[i].start()
            own_copies[i].start()

    gain_ref[0:128, :] = -g1
    gain_ref[128:256, :] = -g2

    @pl.when(s > 0)
    def _():
        for i in range(4):
            far_copies[i].wait_send()
            own_copies[i].wait_send()


def root_kernel(expected_input, state_map, input_map, cost_input, gain_ref):
    y = split(expected_input[...])
    huu = dot_split(split(input_map[...].T), y) + eye_times(cost_input[0:1, :], 256)
    hux = dot_split(y, split(state_map[...]), CONTRACT_ROWS)
    hux1, th, rest, g2, g1 = solve(huu, hux, inverse128)
    gain_ref[0:128, :] = -g1
    gain_ref[128:256, :] = -g2


def on_device(
    state_map, input_map, cost_state, cost_input, terminal, prob_num, crosses,
    root_state_map, root_input_map, root_cost_input, root_terminal,
):
    sections, groups = lax.axis_size("section"), lax.axis_size("leaf")
    section, leaf = lax.axis_index("section"), lax.axis_index("leaf")
    nx, nu = input_map.shape[1], input_map.shape[2]
    vmem, smem = pl.BlockSpec(memory_space=pltpu.VMEM), pl.BlockSpec(memory_space=pltpu.SMEM)
    dma = pltpu.SemaphoreType.DMA((4,))
    hess, gain = pl.pallas_call(
        functools.partial(chain_kernel, sections, groups),
        out_shape=(jax.ShapeDtypeStruct((nx, nx), F32), jax.ShapeDtypeStruct((nu, nx), F32)),
        in_specs=[smem, smem] + [vmem] * 5,
        out_specs=(vmem, vmem),
        scratch_shapes=[VMEM((nx, nx), F32)] * 4
        + [
            VMEM((2, nx, nx), BF16), VMEM((2, nx, nu), BF16), VMEM((2, nx, nx), BF16), VMEM((2, nu, nx), BF16),
            VMEM((2, nx, nx), BF16), VMEM((2, nx, nx), BF16), VMEM((2, nx, nu), BF16),
            VMEM((nu, nx), F32), VMEM((2, nu, nx), BF16), VMEM((2, nu, nx), BF16), VMEM((128, 128), F32),
        ]
        + [dma] * 4,
        compiler_params=pltpu.CompilerParams(collective_id=0, has_side_effects=True, vmem_limit_bytes=60 << 20),
    )(
        prob_num.reshape(1), crosses.reshape(1), state_map[0], input_map[0],
        cost_state.reshape(1, nx), cost_input.reshape(1, nu), terminal.reshape(1, nx),
    )
    precise = lax.Precision.HIGHEST
    weight = jnp.where(section == 0, prob_num[0, 0, 0].astype(F32) / 64.0, 0.0)
    part = jnp.dot(hess * weight, root_input_map, precision=precise)
    total = lax.psum(part, ("section", "leaf")) + root_terminal[0][:, None] * root_input_map
    root = pl.pallas_call(
        root_kernel,
        out_shape=jax.ShapeDtypeStruct((nu, nx), F32),
        in_specs=[vmem] * 4,
        out_specs=vmem,
        compiler_params=pltpu.CompilerParams(vmem_limit_bytes=60 << 20),
    )(total, root_state_map, root_input_map, root_cost_input)
    mine = lax.dynamic_slice_in_dim(root, section * (nu // sections), nu // sections, 0)
    return hess[None, None, None], gain[None, None, None], mine[None]


def solution(mesh):
    in_specs = (
        P("section", None, None), P("section", None, None), P("section", None, "leaf", None),
        P("section", None, "leaf", None), P("section", None, "leaf", None), P("section", None, "leaf"),
        P("section", None, "leaf"), P(), P(), P(), P(),
    )
    out_specs = (
        P("section", None, "leaf", None, None), P("section", None, "leaf", None, None), P(None, "section", None),
    )
    return jax.shard_map(on_device, mesh=mesh, in_specs=in_specs, out_specs=out_specs, check_vma=False)
```

time: 1290 us -> 465 us (0.36)
  waiting for transfers between devices: 986 us -> 252 us
  Pallas kernels: 0 us -> 189 us
  other arithmetic: 135 us -> 1.97 us
  loops' own time: 68.3 us -> 0 us
  local copies, waits for them, and re-layouts: 35 us -> 3.68 us
  matrix products: 24.6 us -> 3.02 us
    ppermute x15 -> x0, waiting for transfers between devices: 730 us -> none  [the longest x8 608 us: shifted(): return lax.ppermute(array, axis, pairs)]
    pallas_call x0 -> x2, Pallas kernels: none -> 189 us  [the longest x1 177 us: on_device(): pl.pallas_call(functools.partial(chain_kernel, sections, groups), out_sha...]
    another operation x20 -> x0, other arithmetic: 108 us -> none  [the longest x12 68.6 us: finish(): factor = jnp.linalg.cholesky(hess_uu)]
    another operation x10 -> x0, loops' own time: 68.3 us -> none  [the longest x8 68.3 us: on_device(): lax.cond(active, compute_node, keep_buffers, (hess_out, gain_out))]
    another operation x29 -> x0, local copies, waits for them, and re-layouts: 26.1 us -> none
    mul x14 -> x0, other arithmetic: 21.8 us -> none  [the longest x7 12.5 us: on_device(): far_part = arrived_flag[0] * arrived]
    dot_general x10 -> x1, matrix products: 18.5 us -> 3.02 us  [on_device(): part = jnp.dot(hess * weight, root_input_map, precision=precise)]
  transfers between devices with their start and end apart: 16 -> 1, of which waited for: 15 -> 1; matrix products, arithmetic and copies ran while one was open for 0% -> 0% of each run, Pallas kernels for 0% -> 0%
where the time goes in v1:
time: 465 us
  waiting for transfers between devices  252 us (54%)
  Pallas kernels  189 us (41%)
  between operations  15.4 us (3%)
    psum x1, waiting for transfers between devices, on_device(): lax.psum(part, ('section', 'leaf'))  252 us
    pallas_call x1, Pallas kernels, on_device(): pl.pallas_call(functools.partial(chain_kernel, sections, groups), out_sha...  177 us
    pallas_call x1, Pallas kernels, on_device(): pl.pallas_call(root_kernel, out_shape=jax.ShapeDtypeStruct((nu, nx), F32)...  11.4 us
  transfers between devices with their start and end apart: 1, of which 1 were waited for; matrix products, arithmetic and copies ran while one was open for 0% of the time, Pallas kernels for 0%

profile of v1, /device:TPU:2, one launch (start us, length us, event | category | flops | bytes accessed | tf_op | source)
XLA Modules:
  0.0 465.1 jit_solution(1600871243400216321)
XLA Ops:
  7.2 0.0 all-reduce.2.cloned.1.call-start
  8.5 0.0 copy-start
  8.5 177.2 %shard_map.130 = (f32[512,512]{1,0:T(8,128)}, f32[256,512]{1,0:T(8,128)}) custom-call(s32[1]{0:T(128)} %bitcast.14.prob, s32[1]{0:T(128)} %bitcast.15.crosses, f32[512,512]{1,0:T(8,128)} %bitcast.17, f32[512,256]{1,0:T(8,128)} %bitcast.18, f32[1,512]{1,0:T(1,128)} %bitcast.20, f32[1,256]{1,0:T(1,128)} %bitcast.23, f32[1,512]{1,0:T(1,128)} %bitcast.21), custom_call_target="tpu_custom_call" | custom-call | tf_op jit(solution)/shard_map/pallas_call | solution.py:230
  185.7 0.0 copy-done
  185.7 3.0 fusion
  188.8 0.0 all-reduce.2.cloned.1.call-update
  188.8 0.0 copy-start.3
  188.8 252.3 %all-reduce.2.cloned.1.call-done = f32[512,256]{1,0:T(8,128)} async-done(((f32[512,256]{1,0:T(8,128)}), f32[512,256]{1,0:T(8,128)}) %all-reduce.2.cloned.1.call-update) | async-done | bytes 524304 | tf_op jit(solution)/shard_map/psum | solution.py:250
  441.1 0.0 copy-done.3
  441.1 2.0 multiply_add_fusion.expected_input
  443.1 0.0 copy-start.1
  443.1 11.4 %shard_map.131 = f32[256,512]{1,0:T(8,128)} custom-call(f32[512,256]{1,0:T(8,128)} %multiply_add_fusion.expected_input, f32[512,512]{1,0:T(8,128)} %state_map.1, f32[512,256]{1,0:T(8,128)} %input_map.1, f32[1,256]{1,0:T(1,128)} %cost_input.1), custom_call_target="tpu_custom_call" | custom-call | tf_op jit(solution)/shard_map/pallas_call | solution.py:251
  454.5 1.5 dynamic-slice_bitcast_fusion
  456.0 0.0 copy-done.1
  456.0 0.0 copy-start.2
  456.0 1.0 copy.19
  457.0 0.4 copy-done.2
  457.4 0.8 copy.20
Async XLA Ops:
  7.2 434.0 %all-reduce.2.cloned.1.call-start = ((), (), s32[]{:S(2)}) async-start(), calls=%async_computation | async-start | bytes 1048576 | tf_op jit(solution)/shard_map/psum | solution.py:250
  8.5 177.2 %copy-start = (f32[512,256]{1,0:T(8,128)S(1)}, f32[512,256]{1,0:T(8,128)}, u32[]{:S(2)}) copy-start(f32[512,256]{1,0:T(8,128)} %input_map.1) | copy-start | bytes 1572868
  188.8 252.3 %copy-start.3 = (f32[1,512]{1,0:T(1,128)S(1)}, f32[1,512]{1,0:T(1,128)}, u32[]{:S(2)}) copy-start(f32[1,512]{1,0:T(1,128)} %param.21) | copy-start | bytes 6148
  443.1 12.9 %copy-start.1 = (f32[512,512]{1,0:T(8,128)S(1)}, f32[512,512]{1,0:T(8,128)}, u32[]{:S(2)}) copy-start(f32[512,512]{1,0:T(8,128)} %get-tuple-element.5) | copy-start | bytes 3145732
  456.0 1.4 copy-start.2
Sparse Core Ops, SparseCore 0:
  188.9 252.1 all-reduce.1

commit v2 on v1

--- a/solution.py
+++ b/solution.py
@@ -92,10 +92,13 @@
 
 def chain_kernel(
     sections, groups, prob, crosses, state_map, input_map, cost_state, cost_input, terminal,
-    hess_ref, gain_ref,
-    own_in, far_in, own_out, far_out,
-    m_s, n_s, mt_s, nt_s, e_s, ym_s, yn_s, hux_ref, z_ref, x_ref, inv_ref,
+    root_state_map, root_input_map, root_cost_input, root_terminal,
+    hess_hbm, gain_hbm, root_ref,
+    hess_ref, gain_ref, own_in, far_in, own_out, far_out,
+    m_s, n_s, mt_s, nt_s, e_s, ym_s, yn_s, hux_ref, z_ref, x_ref,
+    mr_ref, nr_ref, mr_s, nr_s, nrt_s, tail_ref, part_ref, parts_in, full_ref, slice_ref,
     own_send, own_recv, far_send, far_recv,
+    part_send, part_recv, full_send, full_recv, slice_send, slice_recv, local,
 ):
     s = lax.axis_index("section")
     g = lax.axis_index("leaf")
@@ -107,7 +110,24 @@
     barrier = pltpu.get_barrier_semaphore()
     for other in parents + children:
         pl.semaphore_signal(barrier, inc=1, device_id=other, device_id_type=MESH)
-    pl.semaphore_wait(barrier, 4)
+
+    @pl.when(s == 0)
+    def _():
+        @pl.loop(1, groups)
+        def _(d):
+            pl.semaphore_signal(
+                barrier, inc=1, device_id={"leaf": lax.rem(g + d, groups)}, device_id_type=MESH
+            )
+
+        @pl.loop(1, sections)
+        def _(d):
+            pl.semaphore_signal(barrier, inc=1, device_id={"section": d}, device_id_type=MESH)
+
+    @pl.when(s > 0)
+    def _():
+        pl.semaphore_signal(barrier, inc=1, device_id={"section": 0}, device_id_type=MESH)
+
+    pl.semaphore_wait(barrier, jnp.where(s == 0, 4 + (groups - 1) + (sections - 1), 5))
 
     def slabs(src, dst, send, recv, device):
         out = []
@@ -133,6 +153,23 @@
         n_s[0, block, :], n_s[1, block, :] = split(value)
         nt_s[0, :, block], nt_s[1, :, block] = split(value.T)
 
+    @pl.when(s == 0)
+    def _():
+        fetch_m = pltpu.make_async_copy(root_state_map, mr_ref, local.at[0])
+        fetch_n = pltpu.make_async_copy(root_input_map, nr_ref, local.at[1])
+        fetch_m.start()
+        fetch_n.start()
+        fetch_m.wait()
+        fetch_n.wait()
+        for i in range(4):
+            block = slice(128 * i, 128 * (i + 1))
+            mr_s[0, block, :], mr_s[1, block, :] = split(mr_ref[block, :])
+            value = nr_ref[block, :]
+            nr_s[0, block, :], nr_s[1, block, :] = split(value)
+            nrt_s[0, :, block], nrt_s[1, :, block] = split(value.T)
+            column = jnp.sum(eye_times(root_terminal[0:1, block], 128), axis=1, keepdims=True)
+            tail_ref[block, :] = column * value
+
     @pl.when(s == sections - 1)
     def _():
         own_in[...] = jnp.zeros_like(own_in)
@@ -163,17 +200,15 @@
     huu = dot_split(nt, (yn_s[0], yn_s[1])) + eye_times(cost_input[0:1, :], 256)
     for j in range(2):
         colb = slice(256 * j, 256 * (j + 1))
-        ym = (ym_s[0, :, colb], ym_s[1, :, colb])
-        hux_ref[:, colb] = dot_split(nt, ym)
-        hess_ref[:, colb] = dot_split(mt, ym)
-    for i in range(4):
-        block = slice(128 * i, 128 * (i + 1))
-        hess_ref[block, block] = hess_ref[block, block] + eye_times(cost_state[0:1, block], 128)
-
-    def inv(a):
-        return inverse128(a)
-
-    hux1, th, rest, g2, g1 = solve(huu, hux_ref[...], inv)
+        hux_ref[:, colb] = dot_split(nt, (ym_s[0, :, colb], ym_s[1, :, colb]))
+    for i in range(2):
+        rowb = slice(256 * i, 256 * (i + 1))
+        colb = slice(0, 256 * (i + 1))
+        hess_ref[rowb, colb] = dot_split(
+            (mt_s[0, rowb, :], mt_s[1, rowb, :]), (ym_s[0, :, colb], ym_s[1, :, colb])
+        )
+
+    hux1, th, rest, g2, g1 = solve(huu, hux_ref[...], inverse128)
     x_ref[0, 0:128, :], x_ref[1, 0:128, :] = split(hux1)
     x_ref[0, 128:256, :], x_ref[1, 128:256, :] = split(rest)
     z_ref[0, 0:128, :], z_ref[1, 0:128, :] = split(th)
@@ -182,25 +217,44 @@
     crossing = crosses[0].astype(F32)
     far_weight = weight * crossing
     own_weight = weight - far_weight
-    for j in range(2):
-        colb = slice(256 * j, 256 * (j + 1))
-        z = (z_ref[0, :, colb], z_ref[1, :, colb])
-        hess_ref[:, colb] = hess_ref[:, colb] - dot_split((x_ref[0], x_ref[1]), z, CONTRACT_ROWS)
+
+    for i in range(2):
+        rowc = slice(256 * i, 256 * (i + 1))
+        colc = slice(0, 256 * (i + 1))
+        update = dot_split(
+            (x_ref[0, :, rowc], x_ref[1, :, rowc]), (z_ref[0, :, colc], z_ref[1, :, colc]), CONTRACT_ROWS
+        )
+        for h in range(2):
+            k = 2 * i + h
+            rowb, colb = slice(128 * k, 128 * (k + 1)), slice(0, 128 * (k + 1))
+            value = hess_ref[rowb, colb] - update[128 * h : 128 * (h + 1), 0 : 128 * (k + 1)]
+            hess_ref[rowb, colb] = value
+            diagonal = value[:, 128 * k :] + eye_times(cost_state[0:1, rowb], 128)
+            hess_ref[rowb, rowb] = diagonal
+            if k > 0:
+                below = value[:, 0 : 128 * k]
+                far_out[rowb, 0 : 128 * k] = below * far_weight
+                own_out[rowb, 0 : 128 * k] = below * own_weight
+            far_out[rowb, rowb] = diagonal * far_weight
+            own_out[rowb, rowb] = diagonal * own_weight
+        for k in (2 * i, 2 * i + 1):
+            @pl.when(s > 0)
+            def _():
+                far_copies[k].start()
+                own_copies[k].start()
 
     for i in range(4):
         rowb = slice(128 * i, 128 * (i + 1))
-        colb = slice(0, 128 * (i + 1))
-        value = hess_ref[rowb, colb]
-        far_out[rowb, colb] = value * far_weight
-        own_out[rowb, colb] = value * own_weight
-
-        @pl.when(s > 0)
-        def _():
-            far_copies[i].start()
-            own_copies[i].start()
-
+        for j in range(i):
+            colb = slice(128 * j, 128 * (j + 1))
+            hess_ref[colb, rowb] = hess_ref[rowb, colb].T
     gain_ref[0:128, :] = -g1
     gain_ref[128:256, :] = -g2
+
+    hess_write = pltpu.make_async_copy(hess_ref, hess_hbm, local.at[2])
+    gain_write = pltpu.make_async_copy(gain_ref, gain_hbm, local.at[3])
+    hess_write.start()
+    gain_write.start()
 
     @pl.when(s > 0)
     def _():
@@ -208,14 +262,95 @@
             far_copies[i].wait_send()
             own_copies[i].wait_send()
 
-
-def root_kernel(expected_input, state_map, input_map, cost_input, gain_ref):
-    y = split(expected_input[...])
-    huu = dot_split(split(input_map[...].T), y) + eye_times(cost_input[0:1, :], 256)
-    hux = dot_split(y, split(state_map[...]), CONTRACT_ROWS)
-    hux1, th, rest, g2, g1 = solve(huu, hux, inverse128)
-    gain_ref[0:128, :] = -g1
-    gain_ref[128:256, :] = -g2
+    chunk = part_ref.shape[0] // groups
+
+    def part_copy(peer, sender):
+        return pltpu.make_async_remote_copy(
+            src_ref=part_ref.at[pl.ds(pl.multiple_of(chunk * peer, chunk), chunk), :], dst_ref=parts_in.at[sender],
+            send_sem=part_send.at[peer], recv_sem=part_recv.at[sender],
+            device_id={"leaf": peer}, device_id_type=MESH,
+        )
+
+    def full_copy(peer, sender):
+        here = (pl.ds(pl.multiple_of(chunk * sender, chunk), chunk), slice(None))
+        return pltpu.make_async_remote_copy(
+            src_ref=full_ref.at[here], dst_ref=full_ref.at[here],
+            send_sem=full_send.at[peer], recv_sem=full_recv.at[sender],
+            device_id={"leaf": peer}, device_id_type=MESH,
+        )
+
+    def slice_copy(other):
+        return pltpu.make_async_remote_copy(
+            src_ref=gain_ref.at[pl.ds(pl.multiple_of(32 * other, 32), 32), :], dst_ref=slice_ref,
+            send_sem=slice_send.at[other], recv_sem=slice_recv.at[0],
+            device_id={"section": other}, device_id_type=MESH,
+        )
+
+    @pl.when(s == 0)
+    def _():
+        nr = (nr_s[0], nr_s[1])
+        for i in range(2):
+            rowb = slice(256 * i, 256 * (i + 1))
+            part_ref[rowb, :] = dot_split(split(hess_ref[rowb, :]), nr) * weight
+
+        @pl.loop(1, groups)
+        def _(d):
+            part_copy(lax.rem(g + d, groups), g).start()
+
+        mine = pl.ds(pl.multiple_of(chunk * g, chunk), chunk)
+        parts_in[g] = part_ref[mine, :]
+
+        @pl.loop(1, groups)
+        def _(d):
+            peer = lax.rem(g + d, groups)
+            part_copy(peer, peer).wait_recv()
+
+        total = tail_ref[mine, :]
+        for i in range(groups):
+            total = total + parts_in[i]
+        full_ref[mine, :] = total
+
+        @pl.loop(1, groups)
+        def _(d):
+            full_copy(lax.rem(g + d, groups), g).start()
+
+        gain_write.wait()
+
+        @pl.loop(1, groups)
+        def _(d):
+            peer = lax.rem(g + d, groups)
+            full_copy(peer, peer).wait_recv()
+
+        y = split(full_ref[...])
+        root_huu = dot_split((nrt_s[0], nrt_s[1]), y) + eye_times(root_cost_input[0:1, :], 256)
+        root_hux = dot_split(y, (mr_s[0], mr_s[1]), CONTRACT_ROWS)
+        _, _, _, low, high = solve(root_huu, root_hux, inverse128)
+        gain_ref[0:128, :] = -high
+        gain_ref[128:256, :] = -low
+
+        @pl.loop(1, sections)
+        def _(d):
+            slice_copy(d).start()
+
+        root_ref[...] = gain_ref[0:32, :]
+
+        @pl.loop(1, groups)
+        def _(d):
+            peer = lax.rem(g + d, groups)
+            part_copy(peer, g).wait_send()
+            full_copy(peer, g).wait_send()
+
+        @pl.loop(1, sections)
+        def _(d):
+            slice_copy(d).wait_send()
+
+    @pl.when(s > 0)
+    def _():
+        gain_write.wait()
+        slice_copy(s).wait_recv()
+        root_ref[...] = slice_ref[...]
+
+    hess_write.wait()
 
 
 def on_device(
@@ -223,39 +358,38 @@
     root_state_map, root_input_map, root_cost_input, root_terminal,
 ):
     sections, groups = lax.axis_size("section"), lax.axis_size("leaf")
-    section, leaf = lax.axis_index("section"), lax.axis_index("leaf")
     nx, nu = input_map.shape[1], input_map.shape[2]
     vmem, smem = pl.BlockSpec(memory_space=pltpu.VMEM), pl.BlockSpec(memory_space=pltpu.SMEM)
-    dma = pltpu.SemaphoreType.DMA((4,))
-    hess, gain = pl.pallas_call(
+    hbm = pl.BlockSpec(memory_space=pl.ANY)
+    dma = pltpu.SemaphoreType.DMA
+    hess, gain, mine = pl.pallas_call(
         functools.partial(chain_kernel, sections, groups),
-        out_shape=(jax.ShapeDtypeStruct((nx, nx), F32), jax.ShapeDtypeStruct((nu, nx), F32)),
-        in_specs=[smem, smem] + [vmem] * 5,
-        out_specs=(vmem, vmem),
-        scratch_shapes=[VMEM((nx, nx), F32)] * 4
+        out_shape=(
+            jax.ShapeDtypeStruct((nx, nx), F32),
+            jax.ShapeDtypeStruct((nu, nx), F32),
+            jax.ShapeDtypeStruct((nu // sections, nx), F32),
+        ),
+        in_specs=[smem, smem] + [vmem] * 5 + [hbm, hbm, vmem, vmem],
+        out_specs=(hbm, hbm, vmem),
+        scratch_shapes=[VMEM((nx, nx), F32), VMEM((nu, nx), F32)]
+        + [VMEM((nx, nx), F32)] * 4
         + [
             VMEM((2, nx, nx), BF16), VMEM((2, nx, nu), BF16), VMEM((2, nx, nx), BF16), VMEM((2, nu, nx), BF16),
             VMEM((2, nx, nx), BF16), VMEM((2, nx, nx), BF16), VMEM((2, nx, nu), BF16),
-            VMEM((nu, nx), F32), VMEM((2, nu, nx), BF16), VMEM((2, nu, nx), BF16), VMEM((128, 128), F32),
+            VMEM((nu, nx), F32), VMEM((2, nu, nx), BF16), VMEM((2, nu, nx), BF16),
+            VMEM((nx, nx), F32), VMEM((nx, nu), F32), VMEM((2, nx, nx), BF16), VMEM((2, nx, nu), BF16),
+            VMEM((2, nu, nx), BF16), VMEM((nx, nu), F32), VMEM((nx, nu), F32),
+            VMEM((groups, nx // groups, nu), F32), VMEM((nx, nu), F32), VMEM((nu // sections, nx), F32),
         ]
-        + [dma] * 4,
+        + [dma((4,))] * 4
+        + [dma((groups,))] * 4
+        + [dma((sections,)), dma((1,)), dma((4,))],
         compiler_params=pltpu.CompilerParams(collective_id=0, has_side_effects=True, vmem_limit_bytes=60 << 20),
     )(
         prob_num.reshape(1), crosses.reshape(1), state_map[0], input_map[0],
         cost_state.reshape(1, nx), cost_input.reshape(1, nu), terminal.reshape(1, nx),
+        root_state_map, root_input_map, root_cost_input, root_terminal,
     )
-    precise = lax.Precision.HIGHEST
-    weight = jnp.where(section == 0, prob_num[0, 0, 0].astype(F32) / 64.0, 0.0)
-    part = jnp.dot(hess * weight, root_input_map, precision=precise)
-    total = lax.psum(part, ("section", "leaf")) + root_terminal[0][:, None] * root_input_map
-    root = pl.pallas_call(
-        root_kernel,
-        out_shape=jax.ShapeDtypeStruct((nu, nx), F32),
-        in_specs=[vmem] * 4,
-        out_specs=vmem,
-        compiler_params=pltpu.CompilerParams(vmem_limit_bytes=60 << 20),
-    )(total, root_state_map, root_input_map, root_cost_input)
-    mine = lax.dynamic_slice_in_dim(root, section * (nu // sections), nu // sections, 0)
     return hess[None, None, None], gain[None, None, None], mine[None]
 
 

time: 465 us -> 217 us (0.47)
  waiting for transfers between devices: 252 us -> 0 us
  Pallas kernels: 189 us -> 210 us
  between operations: 15.4 us -> 1.94 us
    psum x1 -> x0, waiting for transfers between devices: 252 us -> none  [on_device(): lax.psum(part, ('section', 'leaf'))]
    pallas_call x1, Pallas kernels: 177 us -> 210 us  [on_device(): pl.pallas_call(functools.partial(chain_kernel, sections, groups), out_sha...]
    pallas_call x1 -> x0, Pallas kernels: 11.4 us -> none  [on_device(): pl.pallas_call(root_kernel, out_shape=jax.ShapeDtypeStruct((nu, nx), F32)...]
  transfers between devices with their start and end apart: 1 -> 0, of which waited for: 1 -> 0; matrix products, arithmetic and copies ran while one was open for 0% -> 0% of each run, Pallas kernels for 0% -> 0%
where the time goes in v2:
time: 217 us; the launch traced here: 216 us
  Pallas kernels  210 us (97%)
  local copies, waits for them, and re-layouts  3.82 us (2%)
    pallas_call x1, Pallas kernels, on_device(): pl.pallas_call(functools.partial(chain_kernel, sections, groups), out_sha...  210 us

profile of v2, /device:TPU:2, one launch (start us, length us, event | category | flops | bytes accessed | tf_op | source)
XLA Modules:
  0.0 215.6 jit_solution(9978955757718046373)
XLA Ops:
  1.9 209.9 %shard_map.130 = (f32[512,512]{1,0:T(8,128)}, f32[256,512]{1,0:T(8,128)}, f32[32,512]{1,0:T(8,128)}) custom-call(s32[1]{0:T(128)} %bitcast.10.prob, s32[1]{0:T(128)} %bitcast.11.crosses, f32[512,512]{1,0:T(8,128)} %bitcast.12, f32[512,256]{1,0:T(8,128)} %bitcast.15, f32[1,512]{1,0:T(1,128)} %bitcast.17, f32[1,256]{1,0:T(1,128)} %bitcast.19, ...), custom_call_target="tpu_custom_call" | custom-call | tf_op jit(solution)/shard_map/pallas_call | solution.py:365
  211.8 0.0 copy-start
  211.8 2.3 %copy.19 = f32[1,1,1,512,512]{4,3,2,1,0:T(8,128)} copy(f32[1,1,1,512,512]{4,3,2,1,0:T(8,128)} %bitcast.13) | data formatting | bytes 2097152
  214.1 0.0 copy-done
  214.1 0.0 copy-start.1
  214.1 0.8 copy.20
  214.9 0.1 copy-done.1
  215.0 0.6 copy.21
Async XLA Ops:
  211.8 2.3 %copy-start = (f32[256,512]{1,0:T(8,128)S(1)}, f32[256,512]{1,0:T(8,128)}, u32[]{:S(2)}) copy-start(f32[256,512]{1,0:T(8,128)} %get-tuple-element.7) | copy-start | bytes 1572868
  214.1 0.9 copy-start.1

commit v3 on v2

--- a/solution.py
+++ b/solution.py
@@ -8,6 +8,11 @@
 from jax.sharding import PartitionSpec as P
 
 F32, BF16 = jnp.float32, jnp.bfloat16
+PIECES = ((0, 264), (264, 256), (520, 256), (776, 264))
+CONTENT = (
+    (("pair", 0, 1), ("one", 1, 0)), (("one", 2, 0), ("one", 2, 1)), (("one", 3, 0), ("one", 3, 1)),
+    (("pair", 2, 3), ("one", 3, 2)),
+)
 MESH = pl.DeviceIdType.MESH
 VMEM = pltpu.VMEM
 CONTRACT = (((1,), (0,)), ((), ()))
@@ -94,10 +99,10 @@
     sections, groups, prob, crosses, state_map, input_map, cost_state, cost_input, terminal,
     root_state_map, root_input_map, root_cost_input, root_terminal,
     hess_hbm, gain_hbm, root_ref,
-    hess_ref, gain_ref, own_in, far_in, own_out, far_out,
+    hess_ref, gain_ref, own_in, far_in, peer_in, own_out, far_out,
     m_s, n_s, mt_s, nt_s, e_s, ym_s, yn_s, hux_ref, z_ref, x_ref,
     mr_ref, nr_ref, mr_s, nr_s, nrt_s, tail_ref, part_ref, parts_in, full_ref, slice_ref,
-    own_send, own_recv, far_send, far_recv,
+    own_send, own_recv, far_send, far_recv, peer_send, peer_recv,
     part_send, part_recv, full_send, full_recv, slice_send, slice_recv, local,
 ):
     s = lax.axis_index("section")
@@ -106,9 +111,11 @@
     after, before = lax.rem(g + 1, groups), lax.rem(g + groups - 1, groups)
     parents = ({"section": up, "leaf": g}, {"section": up, "leaf": after})
     children = ({"section": down, "leaf": g}, {"section": down, "leaf": before})
+    siblings = ({"leaf": after}, {"leaf": before})
+    far_side = lax.rem(s, 2) == 1
 
     barrier = pltpu.get_barrier_semaphore()
-    for other in parents + children:
+    for other in parents + children + siblings:
         pl.semaphore_signal(barrier, inc=1, device_id=other, device_id_type=MESH)
 
     @pl.when(s == 0)
@@ -127,22 +134,20 @@
     def _():
         pl.semaphore_signal(barrier, inc=1, device_id={"section": 0}, device_id_type=MESH)
 
-    pl.semaphore_wait(barrier, jnp.where(s == 0, 4 + (groups - 1) + (sections - 1), 5))
-
-    def slabs(src, dst, send, recv, device):
-        out = []
-        for i in range(4):
-            part = (pl.ds(128 * i, 128), pl.ds(0, 128 * (i + 1)))
-            out.append(
-                pltpu.make_async_remote_copy(
-                    src_ref=src.at[part], dst_ref=dst.at[part], send_sem=send.at[i], recv_sem=recv.at[i],
-                    device_id=device, device_id_type=MESH,
-                )
+    pl.semaphore_wait(barrier, jnp.where(s == 0, 6 + (groups - 1) + (sections - 1), 7))
+
+    def pieces(src, dst, send, recv, device):
+        return [
+            pltpu.make_async_remote_copy(
+                src_ref=src.at[pl.ds(start, size)], dst_ref=dst.at[pl.ds(start, size)],
+                send_sem=send.at[i], recv_sem=recv.at[i], device_id=device, device_id_type=MESH,
             )
-        return out
-
-    own_copies = slabs(own_out, own_in, own_send, own_recv, parents[0])
-    far_copies = slabs(far_out, far_in, far_send, far_recv, parents[1])
+            for i, (start, size) in enumerate(PIECES)
+        ]
+
+    own_copies = pieces(own_out, own_in, own_send, own_recv, parents[0])
+    far_copies = pieces(far_out, far_in, far_send, far_recv, parents[1])
+    peer_copies = pieces(far_out, peer_in, peer_send, peer_recv, siblings[0])
 
     for i in range(4):
         block = slice(128 * i, 128 * (i + 1))
@@ -173,23 +178,42 @@
     @pl.when(s == sections - 1)
     def _():
         own_in[...] = jnp.zeros_like(own_in)
+
+    @pl.when(far_side)
+    def _():
         far_in[...] = jnp.zeros_like(far_in)
 
-    for i in range(4):
+    r = lax.broadcasted_iota(jnp.int32, (128, 128), 0)
+    c = lax.broadcasted_iota(jnp.int32, (128, 128), 1)
+
+    def put(i, j, block):
+        rowb, colb = slice(128 * i, 128 * (i + 1)), slice(128 * j, 128 * (j + 1))
+        if i == j:
+            block = block + eye_times(terminal[0:1, rowb], 128)
+        e_s[0, rowb, colb], e_s[1, rowb, colb] = split(block)
+        if i != j:
+            e_s[0, colb, rowb], e_s[1, colb, rowb] = split(block.T)
+
+    for p, (start, size) in enumerate(PIECES):
         @pl.when(s < sections - 1)
         def _():
-            far_copies[i].wait_recv()
-            own_copies[i].wait_recv()
-
-        rowb = slice(128 * i, 128 * (i + 1))
-        for j in range(i + 1):
-            colb = slice(128 * j, 128 * (j + 1))
-            block = own_in[rowb, colb] + far_in[rowb, colb]
-            if i == j:
-                block = block + eye_times(terminal[0:1, rowb], 128)
-            e_s[0, rowb, colb], e_s[1, rowb, colb] = split(block)
-            if i != j:
-                e_s[0, colb, rowb], e_s[1, colb, rowb] = split(block.T)
+            own_copies[p].wait_recv()
+
+            @pl.when(jnp.logical_not(far_side))
+            def _():
+                far_copies[p].wait_recv()
+
+        for h, (kind, i, j) in enumerate(CONTENT[p]):
+            here = slice(start + 128 * h, start + 128 * (h + 1))
+            block = own_in[here, :] + far_in[here, :]
+            if kind == "pair":
+                spare = slice(start + 256, start + 257)
+                line = own_in[spare, :] + far_in[spare, :]
+                turned = block.T
+                put(i, i, jnp.where(r >= c, block, turned))
+                put(j, j, jnp.where(r < c, block, jnp.where(r > c, turned, line)))
+            else:
+                put(i, j, block)
 
     e = (e_s[0], e_s[1])
     yn_s[0], yn_s[1] = split(dot_split(e, (n_s[0], n_s[1])))
@@ -218,6 +242,10 @@
     far_weight = weight * crossing
     own_weight = weight - far_weight
 
+    def load(start, value):
+        far_out[start : start + value.shape[0], :] = value * far_weight
+        own_out[start : start + value.shape[0], :] = value * own_weight
+
     for i in range(2):
         rowc = slice(256 * i, 256 * (i + 1))
         colc = slice(0, 256 * (i + 1))
@@ -227,21 +255,36 @@
         for h in range(2):
             k = 2 * i + h
             rowb, colb = slice(128 * k, 128 * (k + 1)), slice(0, 128 * (k + 1))
-            value = hess_ref[rowb, colb] - update[128 * h : 128 * (h + 1), 0 : 128 * (k + 1)]
-            hess_ref[rowb, colb] = value
-            diagonal = value[:, 128 * k :] + eye_times(cost_state[0:1, rowb], 128)
-            hess_ref[rowb, rowb] = diagonal
-            if k > 0:
-                below = value[:, 0 : 128 * k]
-                far_out[rowb, 0 : 128 * k] = below * far_weight
-                own_out[rowb, 0 : 128 * k] = below * own_weight
-            far_out[rowb, rowb] = diagonal * far_weight
-            own_out[rowb, rowb] = diagonal * own_weight
-        for k in (2 * i, 2 * i + 1):
-            @pl.when(s > 0)
+            hess_ref[rowb, colb] = hess_ref[rowb, colb] - update[128 * h : 128 * (h + 1), 0 : 128 * (k + 1)]
+            hess_ref[rowb, rowb] = hess_ref[rowb, rowb] + eye_times(cost_state[0:1, rowb], 128)
+        for p in ((0,), (1, 2, 3))[i]:
+            start = PIECES[p][0]
+            for h, (kind, a, b) in enumerate(CONTENT[p]):
+                block = hess_ref[128 * a : 128 * (a + 1), 128 * b : 128 * (b + 1)]
+                if kind == "pair":
+                    first = hess_ref[128 * a : 128 * (a + 1), 128 * a : 128 * (a + 1)]
+                    second = hess_ref[128 * b : 128 * (b + 1), 128 * b : 128 * (b + 1)]
+                    block = jnp.where(r >= c, first, second)
+                    line = jnp.sum(jnp.where(r == c, second, 0.0), axis=0, keepdims=True)
+                    load(start + 256, jnp.broadcast_to(line, (8, 128)))
+                load(start + 128 * h, block)
+
+            @pl.when(far_side)
             def _():
-                far_copies[k].start()
-                own_copies[k].start()
+                far_copies[p].start()
+                own_copies[p].start()
+
+            @pl.when(jnp.logical_not(far_side) & (s > 0))
+            def _():
+                peer_copies[p].start()
+
+    @pl.when(jnp.logical_not(far_side) & (s > 0))
+    def _():
+        for p, (start, size) in enumerate(PIECES):
+            peer_copies[p].wait_recv()
+            here = slice(start, start + size)
+            own_out[here, :] = own_out[here, :] + peer_in[here, :]
+            own_copies[p].start()
 
     for i in range(4):
         rowb = slice(128 * i, 128 * (i + 1))
@@ -258,9 +301,18 @@
 
     @pl.when(s > 0)
     def _():
-        for i in range(4):
-            far_copies[i].wait_send()
-            own_copies[i].wait_send()
+        for copy in own_copies:
+            copy.wait_send()
+
+        @pl.when(far_side)
+        def _():
+            for copy in far_copies:
+                copy.wait_send()
+
+        @pl.when(jnp.logical_not(far_side))
+        def _():
+            for copy in peer_copies:
+                copy.wait_send()
 
     chunk = part_ref.shape[0] // groups
 
@@ -372,7 +424,7 @@
         in_specs=[smem, smem] + [vmem] * 5 + [hbm, hbm, vmem, vmem],
         out_specs=(hbm, hbm, vmem),
         scratch_shapes=[VMEM((nx, nx), F32), VMEM((nu, nx), F32)]
-        + [VMEM((nx, nx), F32)] * 4
+        + [VMEM((1040, 128), F32)] * 5
         + [
             VMEM((2, nx, nx), BF16), VMEM((2, nx, nu), BF16), VMEM((2, nx, nx), BF16), VMEM((2, nu, nx), BF16),
             VMEM((2, nx, nx), BF16), VMEM((2, nx, nx), BF16), VMEM((2, nx, nu), BF16),
@@ -381,7 +433,7 @@
             VMEM((2, nu, nx), BF16), VMEM((nx, nu), F32), VMEM((nx, nu), F32),
             VMEM((groups, nx // groups, nu), F32), VMEM((nx, nu), F32), VMEM((nu // sections, nx), F32),
         ]
-        + [dma((4,))] * 4
+        + [dma((4,))] * 6
         + [dma((groups,))] * 4
         + [dma((sections,)), dma((1,)), dma((4,))],
         compiler_params=pltpu.CompilerParams(collective_id=0, has_side_effects=True, vmem_limit_bytes=60 << 20),

time: 217 us -> 199 us (0.917)
  Pallas kernels: 210 us -> 191 us
    pallas_call x1, Pallas kernels: 210 us -> 191 us  [on_device(): pl.pallas_call(functools.partial(chain_kernel, sections, groups), out_sha...]
where the time goes in v3:
time: 199 us; the launch traced here: 197 us
  Pallas kernels  191 us (96%)
  local copies, waits for them, and re-layouts  3.82 us (2%)
    pallas_call x1, Pallas kernels, on_device(): pl.pallas_call(functools.partial(chain_kernel, sections, groups), out_sha...  191 us

profile of v3, /device:TPU:2, one launch (start us, length us, event | category | flops | bytes accessed | tf_op | source)
XLA Modules:
  0.0 196.7 jit_solution(2861314945588658159)
XLA Ops:
  1.9 190.9 %shard_map.130 = (f32[512,512]{1,0:T(8,128)}, f32[256,512]{1,0:T(8,128)}, f32[32,512]{1,0:T(8,128)}) custom-call(s32[1]{0:T(128)} %bitcast.10.prob, s32[1]{0:T(128)} %bitcast.11.crosses, f32[512,512]{1,0:T(8,128)} %bitcast.12, f32[512,256]{1,0:T(8,128)} %bitcast.15, f32[1,512]{1,0:T(1,128)} %bitcast.17, f32[1,256]{1,0:T(1,128)} %bitcast.19, ...), custom_call_target="tpu_custom_call" | custom-call | tf_op jit(solution)/shard_map/pallas_call | solution.py:417
  192.9 0.0 copy-start
  192.9 2.3 %copy.19 = f32[1,1,1,512,512]{4,3,2,1,0:T(8,128)} copy(f32[1,1,1,512,512]{4,3,2,1,0:T(8,128)} %bitcast.13) | data formatting | bytes 2097152
  195.2 0.0 copy-done
  195.2 0.0 copy-start.1
  195.2 0.8 copy.20
  196.0 0.1 copy-done.1
  196.1 0.6 copy.21
Async XLA Ops:
  192.9 2.3 %copy-start = (f32[256,512]{1,0:T(8,128)S(1)}, f32[256,512]{1,0:T(8,128)}, u32[]{:S(2)}) copy-start(f32[256,512]{1,0:T(8,128)} %get-tuple-element.7) | copy-start | bytes 1572868
  195.2 0.9 copy-start.1

commit v4 on v3

--- a/solution.py
+++ b/solution.py
@@ -100,8 +100,8 @@
     root_state_map, root_input_map, root_cost_input, root_terminal,
     hess_hbm, gain_hbm, root_ref,
     hess_ref, gain_ref, own_in, far_in, peer_in, own_out, far_out,
-    m_s, n_s, mt_s, nt_s, e_s, ym_s, yn_s, hux_ref, z_ref, x_ref,
-    mr_ref, nr_ref, mr_s, nr_s, nrt_s, tail_ref, part_ref, parts_in, full_ref, slice_ref,
+    m_s, n_s, mt_s, nt_s, e_s, ym_s, yn_s, hux_ref, z_ref, x_ref, yb_ref,
+    mr_ref, nr_ref, mr_s, nr_s, nrt_s, tail_ref, part_ref, parts_in, full_ref, slices_ref, slice_ref,
     own_send, own_recv, far_send, far_recv, peer_send, peer_recv,
     part_send, part_recv, full_send, full_recv, slice_send, slice_recv, local,
 ):
@@ -115,8 +115,13 @@
     far_side = lax.rem(s, 2) == 1
 
     barrier = pltpu.get_barrier_semaphore()
-    for other in parents + children + siblings:
+    for other in children + siblings[1:]:
         pl.semaphore_signal(barrier, inc=1, device_id=other, device_id_type=MESH)
+
+    @pl.when(s > 0)
+    def _():
+        pl.semaphore_signal(barrier, inc=1, device_id={"section": 0}, device_id_type=MESH)
+        pl.semaphore_wait(barrier, 3)
 
     @pl.when(s == 0)
     def _():
@@ -126,24 +131,22 @@
                 barrier, inc=1, device_id={"leaf": lax.rem(g + d, groups)}, device_id_type=MESH
             )
 
-        @pl.loop(1, sections)
-        def _(d):
-            pl.semaphore_signal(barrier, inc=1, device_id={"section": d}, device_id_type=MESH)
-
-    @pl.when(s > 0)
-    def _():
-        pl.semaphore_signal(barrier, inc=1, device_id={"section": 0}, device_id_type=MESH)
-
-    pl.semaphore_wait(barrier, jnp.where(s == 0, 6 + (groups - 1) + (sections - 1), 7))
+        pl.semaphore_wait(barrier, 3 + (groups - 1) + (sections - 1))
 
     def pieces(src, dst, send, recv, device):
         return [
             pltpu.make_async_remote_copy(
                 src_ref=src.at[pl.ds(start, size)], dst_ref=dst.at[pl.ds(start, size)],
-                send_sem=send.at[i], recv_sem=recv.at[i], device_id=device, device_id_type=MESH,
+                send_sem=send.at[0], recv_sem=recv.at[i], device_id=device, device_id_type=MESH,
             )
             for i, (start, size) in enumerate(PIECES)
         ]
+
+    def whole(src, dst, send, recv, device):
+        return pltpu.make_async_remote_copy(
+            src_ref=src, dst_ref=dst, send_sem=send.at[0], recv_sem=recv.at[0],
+            device_id=device, device_id_type=MESH,
+        )
 
     own_copies = pieces(own_out, own_in, own_send, own_recv, parents[0])
     far_copies = pieces(far_out, far_in, far_send, far_recv, parents[1])
@@ -186,6 +189,11 @@
     r = lax.broadcasted_iota(jnp.int32, (128, 128), 0)
     c = lax.broadcasted_iota(jnp.int32, (128, 128), 1)
 
+    top, bottom = slice(0, 256), slice(256, 512)
+
+    def both(ref, rowb, colb):
+        return ref[0, rowb, colb], ref[1, rowb, colb]
+
     def put(i, j, block):
         rowb, colb = slice(128 * i, 128 * (i + 1)), slice(128 * j, 128 * (j + 1))
         if i == j:
@@ -215,11 +223,20 @@
             else:
                 put(i, j, block)
 
-    e = (e_s[0], e_s[1])
-    yn_s[0], yn_s[1] = split(dot_split(e, (n_s[0], n_s[1])))
-    for j in range(2):
-        colb = slice(256 * j, 256 * (j + 1))
-        ym_s[0, :, colb], ym_s[1, :, colb] = split(dot_split(e, (m_s[0, :, colb], m_s[1, :, colb])))
+        if p == 2:
+            upper = dot_split(both(e_s, top, slice(None)), both(n_s, slice(None), slice(None)))
+            yn_s[0, top, :], yn_s[1, top, :] = split(upper)
+            yb_ref[:, 512:768] = dot_split(both(e_s, bottom, top), both(n_s, top, slice(None)))
+            for colb in (slice(0, 256), slice(256, 512)):
+                upper = dot_split(both(e_s, top, slice(None)), both(m_s, slice(None), colb))
+                ym_s[0, top, colb], ym_s[1, top, colb] = split(upper)
+                yb_ref[:, colb] = dot_split(both(e_s, bottom, top), both(m_s, top, colb))
+
+    lower = yb_ref[:, 512:768] + dot_split(both(e_s, bottom, bottom), both(n_s, bottom, slice(None)))
+    yn_s[0, bottom, :], yn_s[1, bottom, :] = split(lower)
+    for colb in (slice(0, 256), slice(256, 512)):
+        lower = yb_ref[:, colb] + dot_split(both(e_s, bottom, bottom), both(m_s, bottom, colb))
+        ym_s[0, bottom, colb], ym_s[1, bottom, colb] = split(lower)
     nt, mt = (nt_s[0], nt_s[1]), (mt_s[0], mt_s[1])
     huu = dot_split(nt, (yn_s[0], yn_s[1])) + eye_times(cost_input[0:1, :], 256)
     for j in range(2):
@@ -301,40 +318,34 @@
 
     @pl.when(s > 0)
     def _():
-        for copy in own_copies:
-            copy.wait_send()
+        whole(own_out, own_in, own_send, own_recv, parents[0]).wait_send()
 
         @pl.when(far_side)
         def _():
-            for copy in far_copies:
-                copy.wait_send()
+            whole(far_out, far_in, far_send, far_recv, parents[1]).wait_send()
 
         @pl.when(jnp.logical_not(far_side))
         def _():
-            for copy in peer_copies:
-                copy.wait_send()
-
-    chunk = part_ref.shape[0] // groups
-
-    def part_copy(peer, sender):
+            whole(far_out, peer_in, peer_send, peer_recv, siblings[0]).wait_send()
+
+    def part_copy(src, dst, peer):
         return pltpu.make_async_remote_copy(
-            src_ref=part_ref.at[pl.ds(pl.multiple_of(chunk * peer, chunk), chunk), :], dst_ref=parts_in.at[sender],
-            send_sem=part_send.at[peer], recv_sem=part_recv.at[sender],
+            src_ref=part_ref.at[src], dst_ref=parts_in.at[dst], send_sem=part_send.at[0], recv_sem=part_recv.at[0],
             device_id={"leaf": peer}, device_id_type=MESH,
         )
 
-    def full_copy(peer, sender):
-        here = (pl.ds(pl.multiple_of(chunk * sender, chunk), chunk), slice(None))
+    def full_copy(here, peer):
         return pltpu.make_async_remote_copy(
-            src_ref=full_ref.at[here], dst_ref=full_ref.at[here],
-            send_sem=full_send.at[peer], recv_sem=full_recv.at[sender],
+            src_ref=full_ref.at[here], dst_ref=full_ref.at[here], send_sem=full_send.at[0], recv_sem=full_recv.at[0],
             device_id={"leaf": peer}, device_id_type=MESH,
         )
+
+    others = pl.ds(0, groups - 1)
+    depth = part_ref.shape[1]
 
     def slice_copy(other):
         return pltpu.make_async_remote_copy(
-            src_ref=gain_ref.at[pl.ds(pl.multiple_of(32 * other, 32), 32), :], dst_ref=slice_ref,
-            send_sem=slice_send.at[other], recv_sem=slice_recv.at[0],
+            src_ref=slices_ref.at[other], dst_ref=slice_ref, send_sem=slice_send.at[0], recv_sem=slice_recv.at[0],
             device_id={"section": other}, device_id_type=MESH,
         )
 
@@ -343,66 +354,55 @@
         nr = (nr_s[0], nr_s[1])
         for i in range(2):
             rowb = slice(256 * i, 256 * (i + 1))
-            part_ref[rowb, :] = dot_split(split(hess_ref[rowb, :]), nr) * weight
-
-        @pl.loop(1, groups)
-        def _(d):
-            part_copy(lax.rem(g + d, groups), g).start()
-
-        mine = pl.ds(pl.multiple_of(chunk * g, chunk), chunk)
-        parts_in[g] = part_ref[mine, :]
+            product = dot_split(split(hess_ref[rowb, :]), nr) * weight
+            for j in range(256 // depth):
+                part_ref[i * (256 // depth) + j] = product[depth * j : depth * (j + 1)]
 
         @pl.loop(1, groups)
         def _(d):
             peer = lax.rem(g + d, groups)
-            part_copy(peer, peer).wait_recv()
-
-        total = tail_ref[mine, :]
+            part_copy(peer, g, peer).start()
+
+        parts_in[g] = part_ref[g]
+        part_copy(others, others, siblings[0]["leaf"]).wait_recv()
+        total = tail_ref[pl.ds(pl.multiple_of(depth * g, depth), depth), :]
         for i in range(groups):
             total = total + parts_in[i]
-        full_ref[mine, :] = total
+        full_ref[g] = total
 
         @pl.loop(1, groups)
         def _(d):
-            full_copy(lax.rem(g + d, groups), g).start()
-
-        gain_write.wait()
-
-        @pl.loop(1, groups)
-        def _(d):
-            peer = lax.rem(g + d, groups)
-            full_copy(peer, peer).wait_recv()
-
-        y = split(full_ref[...])
+            full_copy(g, lax.rem(g + d, groups)).start()
+
+        full_copy(others, siblings[0]["leaf"]).wait_recv()
+        y = split(full_ref[...].reshape(groups * depth, full_ref.shape[2]))
         root_huu = dot_split((nrt_s[0], nrt_s[1]), y) + eye_times(root_cost_input[0:1, :], 256)
         root_hux = dot_split(y, (mr_s[0], mr_s[1]), CONTRACT_ROWS)
         _, _, _, low, high = solve(root_huu, root_hux, inverse128)
-        gain_ref[0:128, :] = -high
-        gain_ref[128:256, :] = -low
+        for i in range(sections):
+            half, start = (-high, -low)[i // (sections // 2)], 32 * (i % (sections // 2))
+            slices_ref[i] = half[start : start + 32]
 
         @pl.loop(1, sections)
         def _(d):
             slice_copy(d).start()
 
-        root_ref[...] = gain_ref[0:32, :]
-
-        @pl.loop(1, groups)
-        def _(d):
-            peer = lax.rem(g + d, groups)
-            part_copy(peer, g).wait_send()
-            full_copy(peer, g).wait_send()
-
-        @pl.loop(1, sections)
-        def _(d):
-            slice_copy(d).wait_send()
+        root_ref[...] = slices_ref[0]
+        part_copy(others, others, siblings[0]["leaf"]).wait_send()
+        full_copy(others, siblings[0]["leaf"]).wait_send()
+        pltpu.make_async_remote_copy(
+            src_ref=slices_ref.at[pl.ds(1, sections - 1)], dst_ref=slices_ref.at[pl.ds(1, sections - 1)],
+            send_sem=slice_send.at[0], recv_sem=slice_recv.at[0],
+            device_id={"section": 1}, device_id_type=MESH,
+        ).wait_send()
 
     @pl.when(s > 0)
     def _():
-        gain_write.wait()
         slice_copy(s).wait_recv()
         root_ref[...] = slice_ref[...]
 
     hess_write.wait()
+    gain_write.wait()
 
 
 def on_device(
@@ -428,14 +428,16 @@
         + [
             VMEM((2, nx, nx), BF16), VMEM((2, nx, nu), BF16), VMEM((2, nx, nx), BF16), VMEM((2, nu, nx), BF16),
             VMEM((2, nx, nx), BF16), VMEM((2, nx, nx), BF16), VMEM((2, nx, nu), BF16),
-            VMEM((nu, nx), F32), VMEM((2, nu, nx), BF16), VMEM((2, nu, nx), BF16),
+            VMEM((nu, nx), F32), VMEM((2, nu, nx), BF16), VMEM((2, nu, nx), BF16), VMEM((nx // 2, nx + nu), F32),
             VMEM((nx, nx), F32), VMEM((nx, nu), F32), VMEM((2, nx, nx), BF16), VMEM((2, nx, nu), BF16),
-            VMEM((2, nu, nx), BF16), VMEM((nx, nu), F32), VMEM((nx, nu), F32),
-            VMEM((groups, nx // groups, nu), F32), VMEM((nx, nu), F32), VMEM((nu // sections, nx), F32),
+            VMEM((2, nu, nx), BF16), VMEM((nx, nu), F32)]
+        + [VMEM((groups, nx // groups, nu), F32)] * 3
+        + [
+            VMEM((sections, nu // sections, nx), F32), VMEM((nu // sections, nx), F32),
         ]
-        + [dma((4,))] * 6
-        + [dma((groups,))] * 4
-        + [dma((sections,)), dma((1,)), dma((4,))],
+        + [dma((1,)), dma((4,))] * 3
+        + [dma((1,))] * 6
+        + [dma((4,))],
         compiler_params=pltpu.CompilerParams(collective_id=0, has_side_effects=True, vmem_limit_bytes=60 << 20),
     )(
         prob_num.reshape(1), crosses.reshape(1), state_map[0], input_map[0],

time: 199 us -> 193 us (0.970)
  Pallas kernels: 191 us -> 186 us
    pallas_call x1, Pallas kernels: 191 us -> 186 us  [on_device(): pl.pallas_call(functools.partial(chain_kernel, sections, groups), out_sha...]
where the time goes in v4:
time: 193 us; the launch traced here: 191 us
  Pallas kernels  186 us (96%)
  local copies, waits for them, and re-layouts  3.82 us (2%)
  between operations  1.94 us (1%)
    pallas_call x1, Pallas kernels, on_device(): pl.pallas_call(functools.partial(chain_kernel, sections, groups), out_sha...  186 us

profile of v4, /device:TPU:2, one launch (start us, length us, event | category | flops | bytes accessed | tf_op | source)
XLA Modules:
  0.0 191.4 jit_solution(7193558753487685982)
XLA Ops:
  1.9 185.6 %shard_map.130 = (f32[512,512]{1,0:T(8,128)}, f32[256,512]{1,0:T(8,128)}, f32[32,512]{1,0:T(8,128)}) custom-call(s32[1]{0:T(128)} %bitcast.10.prob, s32[1]{0:T(128)} %bitcast.11.crosses, f32[512,512]{1,0:T(8,128)} %bitcast.12, f32[512,256]{1,0:T(8,128)} %bitcast.15, f32[1,512]{1,0:T(1,128)} %bitcast.17, f32[1,256]{1,0:T(1,128)} %bitcast.19, ...), custom_call_target="tpu_custom_call" | custom-call | tf_op jit(solution)/shard_map/pallas_call | solution.py:417
  187.6 0.0 copy-start
  187.6 2.3 %copy.19 = f32[1,1,1,512,512]{4,3,2,1,0:T(8,128)} copy(f32[1,1,1,512,512]{4,3,2,1,0:T(8,128)} %bitcast.13) | data formatting | bytes 2097152
  189.9 0.0 copy-done
  189.9 0.0 copy-start.1
  189.9 0.8 copy.20
  190.7 0.1 copy-done.1
  190.8 0.6 copy.21
Async XLA Ops:
  187.6 2.3 %copy-start = (f32[256,512]{1,0:T(8,128)S(1)}, f32[256,512]{1,0:T(8,128)}, u32[]{:S(2)}) copy-start(f32[256,512]{1,0:T(8,128)} %get-tuple-element.7) | copy-start | bytes 1572868
  189.9 0.9 copy-start.1

commit v5 on v4

--- a/solution.py
+++ b/solution.py
@@ -8,10 +8,10 @@
 from jax.sharding import PartitionSpec as P
 
 F32, BF16 = jnp.float32, jnp.bfloat16
-PIECES = ((0, 264), (264, 256), (520, 256), (776, 264))
+PIECES = ((0, 264), (264, 256), (520, 256), (776, 136), (912, 128))
 CONTENT = (
     (("pair", 0, 1), ("one", 1, 0)), (("one", 2, 0), ("one", 2, 1)), (("one", 3, 0), ("one", 3, 1)),
-    (("pair", 2, 3), ("one", 3, 2)),
+    (("pair", 2, 3),), (("one", 3, 2),),
 )
 MESH = pl.DeviceIdType.MESH
 VMEM = pltpu.VMEM
@@ -215,7 +215,7 @@
             here = slice(start + 128 * h, start + 128 * (h + 1))
             block = own_in[here, :] + far_in[here, :]
             if kind == "pair":
-                spare = slice(start + 256, start + 257)
+                spare = slice(start + size - 8, start + size - 7)
                 line = own_in[spare, :] + far_in[spare, :]
                 turned = block.T
                 put(i, i, jnp.where(r >= c, block, turned))
@@ -274,8 +274,8 @@
             rowb, colb = slice(128 * k, 128 * (k + 1)), slice(0, 128 * (k + 1))
             hess_ref[rowb, colb] = hess_ref[rowb, colb] - update[128 * h : 128 * (h + 1), 0 : 128 * (k + 1)]
             hess_ref[rowb, rowb] = hess_ref[rowb, rowb] + eye_times(cost_state[0:1, rowb], 128)
-        for p in ((0,), (1, 2, 3))[i]:
-            start = PIECES[p][0]
+        for p in ((0,), (1, 2, 3, 4))[i]:
+            start, size = PIECES[p]
             for h, (kind, a, b) in enumerate(CONTENT[p]):
                 block = hess_ref[128 * a : 128 * (a + 1), 128 * b : 128 * (b + 1)]
                 if kind == "pair":
@@ -283,7 +283,7 @@
                     second = hess_ref[128 * b : 128 * (b + 1), 128 * b : 128 * (b + 1)]
                     block = jnp.where(r >= c, first, second)
                     line = jnp.sum(jnp.where(r == c, second, 0.0), axis=0, keepdims=True)
-                    load(start + 256, jnp.broadcast_to(line, (8, 128)))
+                    load(start + size - 8, jnp.broadcast_to(line, (8, 128)))
                 load(start + 128 * h, block)
 
             @pl.when(far_side)
@@ -435,7 +435,7 @@
         + [
             VMEM((sections, nu // sections, nx), F32), VMEM((nu // sections, nx), F32),
         ]
-        + [dma((1,)), dma((4,))] * 3
+        + [dma((1,)), dma((len(PIECES),))] * 3
         + [dma((1,))] * 6
         + [dma((4,))],
         compiler_params=pltpu.CompilerParams(collective_id=0, has_side_effects=True, vmem_limit_bytes=60 << 20),

time: 193 us -> 194 us (level)
  no operation moved by 1% of the time
where the time goes in v5:
time: 194 us; the launch traced here: 192 us
  Pallas kernels  187 us (96%)
  local copies, waits for them, and re-layouts  3.82 us (2%)
  between operations  1.94 us (1%)
    pallas_call x1, Pallas kernels, on_device(): pl.pallas_call(functools.partial(chain_kernel, sections, groups), out_sha...  187 us

profile of v5, /device:TPU:2, one launch (start us, length us, event | category | flops | bytes accessed | tf_op | source)
XLA Modules:
  0.0 192.4 jit_solution(1078500730651371841)
XLA Ops:
  1.9 186.6 %shard_map.130 = (f32[512,512]{1,0:T(8,128)}, f32[256,512]{1,0:T(8,128)}, f32[32,512]{1,0:T(8,128)}) custom-call(s32[1]{0:T(128)} %bitcast.10.prob, s32[1]{0:T(128)} %bitcast.11.crosses, f32[512,512]{1,0:T(8,128)} %bitcast.12, f32[512,256]{1,0:T(8,128)} %bitcast.15, f32[1,512]{1,0:T(1,128)} %bitcast.17, f32[1,256]{1,0:T(1,128)} %bitcast.19, ...), custom_call_target="tpu_custom_call" | custom-call | tf_op jit(solution)/shard_map/pallas_call | solution.py:417
  188.5 0.0 copy-start
  188.6 2.3 %copy.19 = f32[1,1,1,512,512]{4,3,2,1,0:T(8,128)} copy(f32[1,1,1,512,512]{4,3,2,1,0:T(8,128)} %bitcast.13) | data formatting | bytes 2097152
  190.9 0.0 copy-done
  190.9 0.0 copy-start.1
  190.9 0.8 copy.20
  191.7 0.1 copy-done.1
  191.7 0.6 copy.21
Async XLA Ops:
  188.5 2.3 %copy-start = (f32[256,512]{1,0:T(8,128)S(1)}, f32[256,512]{1,0:T(8,128)}, u32[]{:S(2)}) copy-start(f32[256,512]{1,0:T(8,128)} %get-tuple-element.7) | copy-start | bytes 1572868
  190.9 0.9 copy-start.1
